TPU v7x, 32 devices: a whole 2x2x4 slice. The times are simulated.
32 devices in a mesh: gx: 4 (over z), gy: 4 (over y, x), gz: 2 (over core).
Axes of the slice: x: 2, y: 2, z: 4, core: 2. Of those that a mesh axis runs over, the one named last changes fastest.
Arguments:
- e_field: float32 [3, 8, 128, 512], P(None, 'gz', 'gx', 'gy'), may hold values from -6 to 6
- h_field: float32 [3, 8, 128, 512], P(None, 'gz', 'gx', 'gy'), may hold values from -6 to 6
- pole_current: float32 [3, 8, 128, 512], P(None, 'gz', 'gx', 'gy'), may hold values from -6 to 6
- material: int32 [8, 128, 512], P('gz', 'gx', 'gy'), may hold values from 0 to 3
- pole_table: float32 [3, 4], replicated, may hold values from 0.2 to 0.9
- cotangent: float32 [16, 8, 4096], P(None, None, ('gx', 'gy', 'gz')), may hold values from -6 to 6
- cosines: float32 [2, 4096], P(None, ('gx', 'gy', 'gz')), may hold values from -0.7 to 0.7
- wavenumber: float32 [16], replicated, may hold values from 0.6 to 0.8
- time_phase: float32 [16], replicated, may hold values from -3.140625 to 3.140625
Outputs:
- e_next: float32 [3, 8, 128, 512], P(None, 'gz', 'gx', 'gy')
- h_next: float32 [3, 8, 128, 512], P(None, 'gz', 'gx', 'gy')
- pole_next: float32 [3, 8, 128, 512], P(None, 'gz', 'gx', 'gy')
All inputs are finite; a program needn't handle non-finite values.
Results may differ from a plain program's by a relative error of at most 0.0003.
Values sent between devices are 32-bit elements; how exact they have to be, the bound alone decides.
No kernel may reach another device: no remote copies, remote signals or barrier semaphores. Data moves between devices by JAX's collectives and lax.ppermute only.
A program may use at most 64 MiB of HBM per device.

v0:
```python
import math
import jax
import jax.numpy as jnp
from jax import lax
from jax.sharding import PartitionSpec as P

FREQS = 16
DIRS = 4096
NPOLE = 4
courant = 0.5


def from_behind(array, axis, by):
    size = lax.axis_size(axis)
    pairs = [(i, i + by) for i in range(size) if 0 <= i + by < size]
    return lax.ppermute(array, axis, pairs)


def surface_source(cotangent, cosines, wavenumber, time_phase, xs, ys):
    count = cotangent.shape[2]
    rows_x = xs.shape[0]
    rows_y = ys.shape[0]

    def one_freq(total, freq):
        wave = wavenumber[freq]
        along_x = wave * cosines[0]
        along_y = wave * cosines[1]
        phase_x = xs[:, None] * along_x[None, :] - time_phase[freq]
        phase_y = ys[:, None] * along_y[None, :]
        cos_x = jnp.cos(phase_x)[None]
        sin_x = jnp.sin(phase_x)[None]
        weights = cotangent[freq]
        real_part = weights[0::2][:, None, :]
        imag_part = weights[1::2][:, None, :]
        first = real_part * cos_x - imag_part * sin_x
        second = -(real_part * sin_x + imag_part * cos_x)
        left = jnp.concatenate([first, second], axis=2).reshape(4 * rows_x, 2 * count)
        right = jnp.concatenate([jnp.cos(phase_y), jnp.sin(phase_y)], axis=1).T
        part = jnp.dot(
            left, right, preferred_element_type=jnp.float32, precision=lax.Precision.HIGHEST
        )
        return (total + part.reshape(4, rows_x, rows_y), None)

    start = jnp.zeros((4, rows_x, rows_y), jnp.float32)
    total, _ = lax.scan(one_freq, start, jnp.arange(cotangent.shape[0], dtype=jnp.int32))
    return total


def ahead(value, nearby, axis):
    rest = lax.slice_in_dim(value, 1, value.shape[axis], axis=axis)
    return jnp.concatenate([rest, nearby], axis) - value


def behind(value, nearby, axis):
    rest = lax.slice_in_dim(value, 0, value.shape[axis] - 1, axis=axis)
    return value - jnp.concatenate([nearby, rest], axis)


def local(
    e_field, h_field, pole_current, material, pole_table, cotangent, cosines, wavenumber, time_phase
):
    depth, width_x, width_y = material.shape
    scale = 1.0 / math.sqrt(DIRS * FREQS)
    anchor_x = (lax.axis_index("gx") * width_x).astype(jnp.float32)
    anchor_y = (lax.axis_index("gy") * width_y).astype(jnp.float32)
    ys = anchor_y + jnp.arange(width_y).astype(jnp.float32)
    first_cot, first_cos = (
        lax.all_gather(cotangent, "gx", axis=2, tiled=True),
        lax.all_gather(cosines, "gx", axis=1, tiled=True),
    )
    band_cot, band_cos = (
        lax.all_gather(first_cot, "gy", axis=2, tiled=True),
        lax.all_gather(first_cos, "gy", axis=1, tiled=True),
    )
    xs = anchor_x + jnp.arange(width_x).astype(jnp.float32)
    partial_value = surface_source(band_cot, band_cos, wavenumber, time_phase, xs, ys)
    source = lax.psum(partial_value, "gz") * scale
    is_top = lax.axis_index("gz") == lax.axis_size("gz") - 1
    top = ((jnp.arange(depth) == depth - 1) & is_top).astype(jnp.float32)[:, None, None]
    next_x = from_behind(e_field[1:3, :, :1, :], "gx", -1)
    next_y = from_behind(e_field[0::2, :, :, :1], "gy", -1)
    next_z = from_behind(e_field[0:2, :1], "gz", -1)
    ex, ey, ez = (e_field[0], e_field[1], e_field[2])
    curl_x = ahead(ez, next_y[1], 2) - ahead(ey, next_z[1], 0)
    curl_y = ahead(ex, next_z[0], 0) - ahead(ez, next_x[1], 1)
    curl_z = ahead(ey, next_x[0], 1) - ahead(ex, next_y[0], 2)
    hx = h_field[0] - courant * curl_x - courant * top * source[2][None]
    hy = h_field[1] - courant * curl_y - courant * top * source[3][None]
    hz = h_field[2] - courant * curl_z
    h_next = jnp.stack([hx, hy, hz])
    prev_x = from_behind(h_next[1:3, :, -1:, :], "gx", 1)
    prev_y = from_behind(h_next[0::2, :, :, -1:], "gy", 1)
    prev_z = from_behind(h_next[0:2, -1:], "gz", 1)
    chosen = (material[None] == jnp.arange(NPOLE, dtype=jnp.int32)[:, None, None, None]).astype(
        jnp.float32
    )
    decay = jnp.sum(chosen * pole_table[0][:, None, None, None], axis=0)
    drive = jnp.sum(chosen * pole_table[1][:, None, None, None], axis=0)
    coef = jnp.sum(chosen * pole_table[2][:, None, None, None], axis=0)
    pole_next = decay[None] * pole_current + drive[None] * e_field
    side_x = behind(hz, prev_y[1], 2) - behind(hy, prev_z[1], 0)
    side_y = behind(hx, prev_z[0], 0) - behind(hz, prev_x[1], 1)
    side_z = behind(hy, prev_x[0], 1) - behind(hx, prev_y[0], 2)
    curl_h = jnp.stack([side_x, side_y, side_z])
    inject = jnp.stack([top * source[0][None], top * source[1][None], jnp.zeros_like(ex)])
    e_next = (
        e_field + coef[None] * (curl_h - 0.5 * (pole_next + pole_current)) - coef[None] * inject
    )
    return (e_next, h_next, pole_next)


def solution(mesh):
    in_specs = (
        P(None, "gz", "gx", "gy"),
        P(None, "gz", "gx", "gy"),
        P(None, "gz", "gx", "gy"),
        P("gz", "gx", "gy"),
        P(),
        P(None, None, ("gx", "gy", "gz")),
        P(None, ("gx", "gy", "gz")),
        P(),
        P(),
    )
    out_specs = (P(None, "gz", "gx", "gy"), P(None, "gz", "gx", "gy"), P(None, "gz", "gx", "gy"))
    return jax.shard_map(local, mesh=mesh, in_specs=in_specs, out_specs=out_specs, check_vma=False)
```

profile of v0, /device:TPU:0, one launch (start us, length us, event | category | flops | bytes accessed | tf_op | source)
XLA Modules:
  0.0 365.0 jit_solution(2642953224590001199)
XLA Ops:
  7.2 17.6 %all_gather.12 = f32[16,8,512]{2,1,0:T(8,128)} all-gather(f32[16,8,128]{2,1,0:T(8,128)} %param.16), channel_id=1, replica_groups=mesh['gx'=4,'gy'=4,'gz'=2] {'gx'}, dimensions={2}, use_global_device_ids=true | all-gather | bytes 327680 | tf_op jit(solution)/shard_map/all_gather | solution.py:68
  27.2 1.4 slice.166
  31.9 10.5 %all_gather.14 = f32[2,512]{1,0:T(2,128)S(1)} all-gather(f32[2,128]{1,0:T(2,128)} %param.17), channel_id=1, replica_groups=mesh['gx'=4,'gy'=4,'gz'=2] {'gx'}, dimensions={1}, use_global_device_ids=true | all-gather | bytes 5120 | tf_op jit(solution)/shard_map/all_gather | solution.py:69
  42.4 10.4 %all_gather.15 = f32[2,2048]{1,0:T(2,128)S(1)} all-gather(f32[2,512]{1,0:T(2,128)S(1)} %all_gather.14), channel_id=1, replica_groups=mesh['gx'=4,'gy'=4,'gz'=2] {'gy'}, dimensions={1}, use_global_device_ids=true | all-gather | bytes 20480 | tf_op jit(solution)/shard_map/all_gather | solution.py:73
  54.8 1.7 select_reduce_fusion.2
  60.4 268.2 %while.11 = (s32[]{:T(128)}, f32[4,32,128]{2,1,0:T(8,128)S(1)}, s32[16]{0:T(128)S(1)}, f32[16,8,2048]{2,1,0:T(8,128)}, f32[16]{0:T(128)}, /*index=5*/f32[2,2048]...) while((s32[]{:T(128)}, f32[4,32,128]{2,1,0:T(8,128)S(1)}, ...), condition=%wide.region_2.3_spmd.clone, body=%wide.region_1.2_spmd.clone.sunk | while | flops 808620352 | bytes 9947153 | solution.py:45
  65.1 1.3 dynamic_slice.25
  66.5 1.7 fusion.56
  70.3 3.7 %multiply_cosine_fusion.2 = (f32[128,2048]{1,0:T(8,128)S(1)}, f32[128,2048]{1,0:T(8,128)S(1)}) fusion(f32[2048]{0:T(1024)S(1)} %bitcast.105, f32[128]{0:T(128)S(1)} %convert_add_fusion.4), kind=kLoop, calls=%fused_computation.10.clone.1 | loop fusion | flops 262144 | bytes 2105856 | tf_op jit(solution)/shard_map/while/body/eval_jaxpr/cos | solution.py:38
  74.0 3.1 fusion.57
  81.9 1.3 dynamic_slice.25
  83.2 1.7 fusion.56
  87.1 3.7 %multiply_cosine_fusion.2 = (f32[128,2048]{1,0:T(8,128)S(1)}, f32[128,2048]{1,0:T(8,128)S(1)}) fusion(f32[2048]{0:T(1024)S(1)} %bitcast.105, f32[128]{0:T(128)S(1)} %convert_add_fusion.4), kind=kLoop, calls=%fused_computation.10.clone.1 | loop fusion | flops 262144 | bytes 2105856 | tf_op jit(solution)/shard_map/while/body/eval_jaxpr/cos | solution.py:38
  90.8 3.1 fusion.57
  100.0 1.7 fusion.56
  103.8 3.7 %multiply_cosine_fusion.2 = (f32[128,2048]{1,0:T(8,128)S(1)}, f32[128,2048]{1,0:T(8,128)S(1)}) fusion(f32[2048]{0:T(1024)S(1)} %bitcast.105, f32[128]{0:T(128)S(1)} %convert_add_fusion.4), kind=kLoop, calls=%fused_computation.10.clone.1 | loop fusion | flops 262144 | bytes 2105856 | tf_op jit(solution)/shard_map/while/body/eval_jaxpr/cos | solution.py:38
  107.5 3.1 fusion.57
  116.8 1.7 fusion.56
  120.6 3.7 %multiply_cosine_fusion.2 = (f32[128,2048]{1,0:T(8,128)S(1)}, f32[128,2048]{1,0:T(8,128)S(1)}) fusion(f32[2048]{0:T(1024)S(1)} %bitcast.105, f32[128]{0:T(128)S(1)} %convert_add_fusion.4), kind=kLoop, calls=%fused_computation.10.clone.1 | loop fusion | flops 262144 | bytes 2105856 | tf_op jit(solution)/shard_map/while/body/eval_jaxpr/cos | solution.py:38
  124.3 3.1 fusion.57
  133.5 1.7 fusion.56
  137.4 3.7 %multiply_cosine_fusion.2 = (f32[128,2048]{1,0:T(8,128)S(1)}, f32[128,2048]{1,0:T(8,128)S(1)}) fusion(f32[2048]{0:T(1024)S(1)} %bitcast.105, f32[128]{0:T(128)S(1)} %convert_add_fusion.4), kind=kLoop, calls=%fused_computation.10.clone.1 | loop fusion | flops 262144 | bytes 2105856 | tf_op jit(solution)/shard_map/while/body/eval_jaxpr/cos | solution.py:38
  141.1 3.1 fusion.57
  149.0 1.3 dynamic_slice.25
  150.3 1.7 fusion.56
  154.1 3.7 %multiply_cosine_fusion.2 = (f32[128,2048]{1,0:T(8,128)S(1)}, f32[128,2048]{1,0:T(8,128)S(1)}) fusion(f32[2048]{0:T(1024)S(1)} %bitcast.105, f32[128]{0:T(128)S(1)} %convert_add_fusion.4), kind=kLoop, calls=%fused_computation.10.clone.1 | loop fusion | flops 262144 | bytes 2105856 | tf_op jit(solution)/shard_map/while/body/eval_jaxpr/cos | solution.py:38
  157.8 3.1 fusion.57
  165.7 1.3 dynamic_slice.25
  167.1 1.7 fusion.56
  170.9 3.7 %multiply_cosine_fusion.2 = (f32[128,2048]{1,0:T(8,128)S(1)}, f32[128,2048]{1,0:T(8,128)S(1)}) fusion(f32[2048]{0:T(1024)S(1)} %bitcast.105, f32[128]{0:T(128)S(1)} %convert_add_fusion.4), kind=kLoop, calls=%fused_computation.10.clone.1 | loop fusion | flops 262144 | bytes 2105856 | tf_op jit(solution)/shard_map/while/body/eval_jaxpr/cos | solution.py:38
  174.6 3.1 fusion.57
  182.5 1.3 dynamic_slice.25
  183.8 1.7 fusion.56
  187.7 3.7 %multiply_cosine_fusion.2 = (f32[128,2048]{1,0:T(8,128)S(1)}, f32[128,2048]{1,0:T(8,128)S(1)}) fusion(f32[2048]{0:T(1024)S(1)} %bitcast.105, f32[128]{0:T(128)S(1)} %convert_add_fusion.4), kind=kLoop, calls=%fused_computation.10.clone.1 | loop fusion | flops 262144 | bytes 2105856 | tf_op jit(solution)/shard_map/while/body/eval_jaxpr/cos | solution.py:38
  191.4 3.1 fusion.57
  200.6 1.7 fusion.56
  204.4 3.7 %multiply_cosine_fusion.2 = (f32[128,2048]{1,0:T(8,128)S(1)}, f32[128,2048]{1,0:T(8,128)S(1)}) fusion(f32[2048]{0:T(1024)S(1)} %bitcast.105, f32[128]{0:T(128)S(1)} %convert_add_fusion.4), kind=kLoop, calls=%fused_computation.10.clone.1 | loop fusion | flops 262144 | bytes 2105856 | tf_op jit(solution)/shard_map/while/body/eval_jaxpr/cos | solution.py:38
  208.1 3.1 fusion.57
  217.4 1.7 fusion.56
  221.2 3.7 %multiply_cosine_fusion.2 = (f32[128,2048]{1,0:T(8,128)S(1)}, f32[128,2048]{1,0:T(8,128)S(1)}) fusion(f32[2048]{0:T(1024)S(1)} %bitcast.105, f32[128]{0:T(128)S(1)} %convert_add_fusion.4), kind=kLoop, calls=%fused_computation.10.clone.1 | loop fusion | flops 262144 | bytes 2105856 | tf_op jit(solution)/shard_map/while/body/eval_jaxpr/cos | solution.py:38
  224.9 3.1 fusion.57
  232.8 1.3 dynamic_slice.25
  234.1 1.7 fusion.56
  238.0 3.7 %multiply_cosine_fusion.2 = (f32[128,2048]{1,0:T(8,128)S(1)}, f32[128,2048]{1,0:T(8,128)S(1)}) fusion(f32[2048]{0:T(1024)S(1)} %bitcast.105, f32[128]{0:T(128)S(1)} %convert_add_fusion.4), kind=kLoop, calls=%fused_computation.10.clone.1 | loop fusion | flops 262144 | bytes 2105856 | tf_op jit(solution)/shard_map/while/body/eval_jaxpr/cos | solution.py:38
  241.7 3.1 fusion.57
  250.9 1.7 fusion.56
  254.7 3.7 %multiply_cosine_fusion.2 = (f32[128,2048]{1,0:T(8,128)S(1)}, f32[128,2048]{1,0:T(8,128)S(1)}) fusion(f32[2048]{0:T(1024)S(1)} %bitcast.105, f32[128]{0:T(128)S(1)} %convert_add_fusion.4), kind=kLoop, calls=%fused_computation.10.clone.1 | loop fusion | flops 262144 | bytes 2105856 | tf_op jit(solution)/shard_map/while/body/eval_jaxpr/cos | solution.py:38
  258.4 3.1 fusion.57
  267.7 1.7 fusion.56
  271.5 3.7 %multiply_cosine_fusion.2 = (f32[128,2048]{1,0:T(8,128)S(1)}, f32[128,2048]{1,0:T(8,128)S(1)}) fusion(f32[2048]{0:T(1024)S(1)} %bitcast.105, f32[128]{0:T(128)S(1)} %convert_add_fusion.4), kind=kLoop, calls=%fused_computation.10.clone.1 | loop fusion | flops 262144 | bytes 2105856 | tf_op jit(solution)/shard_map/while/body/eval_jaxpr/cos | solution.py:38
  275.2 3.1 fusion.57
  284.4 1.7 fusion.56
  288.3 3.7 %multiply_cosine_fusion.2 = (f32[128,2048]{1,0:T(8,128)S(1)}, f32[128,2048]{1,0:T(8,128)S(1)}) fusion(f32[2048]{0:T(1024)S(1)} %bitcast.105, f32[128]{0:T(128)S(1)} %convert_add_fusion.4), kind=kLoop, calls=%fused_computation.10.clone.1 | loop fusion | flops 262144 | bytes 2105856 | tf_op jit(solution)/shard_map/while/body/eval_jaxpr/cos | solution.py:38
  292.0 3.1 fusion.57
  301.2 1.7 fusion.56
  305.0 3.7 %multiply_cosine_fusion.2 = (f32[128,2048]{1,0:T(8,128)S(1)}, f32[128,2048]{1,0:T(8,128)S(1)}) fusion(f32[2048]{0:T(1024)S(1)} %bitcast.105, f32[128]{0:T(128)S(1)} %convert_add_fusion.4), kind=kLoop, calls=%fused_computation.10.clone.1 | loop fusion | flops 262144 | bytes 2105856 | tf_op jit(solution)/shard_map/while/body/eval_jaxpr/cos | solution.py:38
  308.7 3.1 fusion.57
  318.0 1.7 fusion.56
  321.8 3.7 %multiply_cosine_fusion.2 = (f32[128,2048]{1,0:T(8,128)S(1)}, f32[128,2048]{1,0:T(8,128)S(1)}) fusion(f32[2048]{0:T(1024)S(1)} %bitcast.105, f32[128]{0:T(128)S(1)} %convert_add_fusion.4), kind=kLoop, calls=%fused_computation.10.clone.1 | loop fusion | flops 262144 | bytes 2105856 | tf_op jit(solution)/shard_map/while/body/eval_jaxpr/cos | solution.py:38
  325.5 3.1 fusion.57
  330.0 14.3 %all-reduce.2.cloned.1.call-done = f32[4,32,128]{2,1,0:T(8,128)} async-done(((f32[4,32,128]{2,1,0:T(8,128)}), f32[4,32,128]{2,1,0:T(8,128)}) %all-reduce.2.cloned.1.call-update) | async-done | bytes 65552 | tf_op jit(solution)/shard_map/psum | solution.py:77
  347.6 3.7 %collective-permute-start.3 = (f32[2,4,32,1]{3,2,1,0:T(8,128)S(1)}, f32[2,4,32,1]{3,2,1,0:T(8,128)S(1)}, u32[]{:S(2)}, u32[]{:S(2)}) collective-permute-start(f32[2,4,32,1]{3,2,1,0:T(8,128)S(1)} %slice.175), channel_id=1, source_target_pairs={{0,2},{2,4},{4,6},{1,3},{3,5},{5,7},{8,10},{10,12},{12,14},{9,11},... | collective-permute-start | bytes 3080 | tf_op jit(solution)/shard_map/ppermute | solution.py:16
  351.3 3.4 collective-permute-start.5
  354.7 1.6 collective-permute-start.4
  (306 shorter events, 108.4 us)
Async XLA Ops:
  7.2 49.3 %copy-start = (f32[3,4,32,128]{3,2,1,0:T(8,128)S(1)}, f32[3,4,32,128]{3,2,1,0:T(8,128)}, u32[]{:S(2)}) copy-start(f32[3,4,32,128]{3,2,1,0:T(8,128)} %param.11) | copy-start | bytes 589828
  7.2 53.2 %all-gather.2.cloned.1.call-start = ((), (), s32[]{:S(2)}) async-start(), calls=%async_computation | async-start | bytes 1310720 | tf_op jit(solution)/shard_map/all_gather | solution.py:72
  24.9 319.5 %all-reduce.2.cloned.1.call-start = ((), (), s32[]{:S(2)}) async-start(), calls=%async_computation.1 | async-start | bytes 131072 | tf_op jit(solution)/shard_map/psum | solution.py:77
  25.9 33.2 %collective-permute-start.1 = (f32[2,4,32,1]{3,2,1,0:T(8,128)S(1)}, f32[2,4,32,1]{3,2,1,0:T(8,128)S(1)}, u32[]{:S(2)}, u32[]{:S(2)}) collective-permute-start(f32[2,4,32,1]{3,2,1,0:T(8,128)S(1)} %slice.159), channel_id=1, source_target_pairs={{2,0},{4,2},{6,4},{3,1},{5,3},{7,5},{10,8},{12,10},{14,12},{11,9},... | collective-permute-start | bytes 3080 | tf_op jit(solution)/shard_map/ppermute | solution.py:16
  28.5 300.8 %collective-permute-start.2 = (f32[2,1,32,128]{3,2,1,0:T(8,128)}, f32[2,1,32,128]{3,2,1,0:T(8,128)}, u32[]{:S(2)}, u32[]{:S(2)}) collective-permute-start(f32[2,1,32,128]{3,2,1,0:T(8,128)} %slice.166), channel_id=1, source_target_pairs={{1,0},{3,2},{5,4},{7,6},{9,8},{11,10},{13,12},{15,14},{17,16},{19,... | collective-permute-start | bytes 98312 | tf_op jit(solution)/shard_map/ppermute | solution.py:16
  30.6 29.2 %collective-permute-start = (f32[2,4,1,128]{3,2,1,0:T(1,128)S(1)}, f32[2,4,1,128]{3,2,1,0:T(1,128)S(1)}, u32[]{:S(2)}, u32[]{:S(2)}) collective-permute-start(f32[2,4,1,128]{3,2,1,0:T(1,128)S(1)} %slice.155), channel_id=1, source_target_pairs={{8,0},{16,8},{24,16},{9,1},{17,9},{25,17},{10,2},{18,10},{26,18},{... | collective-permute-start | bytes 12296 | tf_op jit(solution)/shard_map/ppermute | solution.py:16
  60.4 4.0 %copy-start.19 = (s32[16]{0:T(128)}, s32[16]{0:T(128)S(1)}, u32[]{:S(2)}) copy-start(s32[16]{0:T(128)S(1)} %get-tuple-element.269) | copy-start | bytes 196 | tf_op jit(solution)/shard_map/while
  74.0 3.1 copy-start.20
  77.1 4.1 %copy-start.19 = (s32[16]{0:T(128)}, s32[16]{0:T(128)S(1)}, u32[]{:S(2)}) copy-start(s32[16]{0:T(128)S(1)} %get-tuple-element.269) | copy-start | bytes 196 | tf_op jit(solution)/shard_map/while
  90.8 3.1 copy-start.20
  93.9 4.1 %copy-start.19 = (s32[16]{0:T(128)}, s32[16]{0:T(128)S(1)}, u32[]{:S(2)}) copy-start(s32[16]{0:T(128)S(1)} %get-tuple-element.269) | copy-start | bytes 196 | tf_op jit(solution)/shard_map/while
  107.5 3.1 copy-start.20
  110.7 4.1 %copy-start.19 = (s32[16]{0:T(128)}, s32[16]{0:T(128)S(1)}, u32[]{:S(2)}) copy-start(s32[16]{0:T(128)S(1)} %get-tuple-element.269) | copy-start | bytes 196 | tf_op jit(solution)/shard_map/while
  124.3 3.1 copy-start.20
  127.4 4.1 %copy-start.19 = (s32[16]{0:T(128)}, s32[16]{0:T(128)S(1)}, u32[]{:S(2)}) copy-start(s32[16]{0:T(128)S(1)} %get-tuple-element.269) | copy-start | bytes 196 | tf_op jit(solution)/shard_map/while
  141.1 3.1 copy-start.20
  144.2 4.1 %copy-start.19 = (s32[16]{0:T(128)}, s32[16]{0:T(128)S(1)}, u32[]{:S(2)}) copy-start(s32[16]{0:T(128)S(1)} %get-tuple-element.269) | copy-start | bytes 196 | tf_op jit(solution)/shard_map/while
  157.8 3.1 copy-start.20
  161.0 4.1 %copy-start.19 = (s32[16]{0:T(128)}, s32[16]{0:T(128)S(1)}, u32[]{:S(2)}) copy-start(s32[16]{0:T(128)S(1)} %get-tuple-element.269) | copy-start | bytes 196 | tf_op jit(solution)/shard_map/while
  174.6 3.1 copy-start.20
  177.7 4.1 %copy-start.19 = (s32[16]{0:T(128)}, s32[16]{0:T(128)S(1)}, u32[]{:S(2)}) copy-start(s32[16]{0:T(128)S(1)} %get-tuple-element.269) | copy-start | bytes 196 | tf_op jit(solution)/shard_map/while
  191.4 3.1 copy-start.20
  194.5 4.1 %copy-start.19 = (s32[16]{0:T(128)}, s32[16]{0:T(128)S(1)}, u32[]{:S(2)}) copy-start(s32[16]{0:T(128)S(1)} %get-tuple-element.269) | copy-start | bytes 196 | tf_op jit(solution)/shard_map/while
  208.1 3.1 copy-start.20
  211.3 4.1 %copy-start.19 = (s32[16]{0:T(128)}, s32[16]{0:T(128)S(1)}, u32[]{:S(2)}) copy-start(s32[16]{0:T(128)S(1)} %get-tuple-element.269) | copy-start | bytes 196 | tf_op jit(solution)/shard_map/while
  224.9 3.1 copy-start.20
  228.0 4.1 %copy-start.19 = (s32[16]{0:T(128)}, s32[16]{0:T(128)S(1)}, u32[]{:S(2)}) copy-start(s32[16]{0:T(128)S(1)} %get-tuple-element.269) | copy-start | bytes 196 | tf_op jit(solution)/shard_map/while
  241.7 3.1 copy-start.20
  244.8 4.1 %copy-start.19 = (s32[16]{0:T(128)}, s32[16]{0:T(128)S(1)}, u32[]{:S(2)}) copy-start(s32[16]{0:T(128)S(1)} %get-tuple-element.269) | copy-start | bytes 196 | tf_op jit(solution)/shard_map/while
  258.4 3.1 copy-start.20
  261.6 4.1 %copy-start.19 = (s32[16]{0:T(128)}, s32[16]{0:T(128)S(1)}, u32[]{:S(2)}) copy-start(s32[16]{0:T(128)S(1)} %get-tuple-element.269) | copy-start | bytes 196 | tf_op jit(solution)/shard_map/while
  275.2 3.1 copy-start.20
  278.3 4.1 %copy-start.19 = (s32[16]{0:T(128)}, s32[16]{0:T(128)S(1)}, u32[]{:S(2)}) copy-start(s32[16]{0:T(128)S(1)} %get-tuple-element.269) | copy-start | bytes 196 | tf_op jit(solution)/shard_map/while
  292.0 3.1 copy-start.20
  295.1 4.1 %copy-start.19 = (s32[16]{0:T(128)}, s32[16]{0:T(128)S(1)}, u32[]{:S(2)}) copy-start(s32[16]{0:T(128)S(1)} %get-tuple-element.269) | copy-start | bytes 196 | tf_op jit(solution)/shard_map/while
  308.7 3.1 copy-start.20
  311.9 4.1 %copy-start.19 = (s32[16]{0:T(128)}, s32[16]{0:T(128)S(1)}, u32[]{:S(2)}) copy-start(s32[16]{0:T(128)S(1)} %get-tuple-element.269) | copy-start | bytes 196 | tf_op jit(solution)/shard_map/while
  325.5 3.1 copy-start.20
  328.6 0.6 copy-start.1
  328.6 17.9 %copy-start.2 = (f32[3,4,32,128]{3,2,1,0:T(8,128)S(1)}, f32[3,4,32,128]{3,2,1,0:T(8,128)}, u32[]{:S(2)}) copy-start(f32[3,4,32,128]{3,2,1,0:T(8,128)} %param.12) | copy-start | bytes 589828
  328.6 17.9 %copy-start.8 = (f32[1,4,32,1]{3,2,1,0:T(8,128)S(1)}, f32[1,4,32,1]{3,2,1,0:T(8,128)}, u32[]{:S(2)}) copy-start(f32[1,4,32,1]{3,2,1,0:T(8,128)} %get-tuple-element.133) | copy-start | bytes 1540
  328.7 17.9 %copy-start.15 = (f32[1,4,1,128]{3,2,1,0:T(1,128)S(1)}, f32[1,4,1,128]{3,2,1,0:T(1,128)}, u32[]{:S(2)}) copy-start(f32[1,4,1,128]{3,2,1,0:T(1,128)} %get-tuple-element.160) | copy-start | bytes 6148
  345.2 1.5 copy-start.7
  346.4 0.8 copy-start.9
  346.4 0.9 copy-start.10
  346.4 0.9 copy-start.11
  346.4 0.9 copy-start.13
  346.4 0.9 copy-start.14
  346.4 0.9 copy-start.16
  346.7 0.8 copy-start.3
  346.7 9.6 %copy-start.18 = (f32[4]{0:T(128)S(1)}, f32[4]{0:T(128)}, u32[]{:S(2)}) copy-start(f32[4]{0:T(128)} %fusion.44) | copy-start | bytes 52
  347.4 9.9 %copy-start.4 = (f32[4,32,128]{2,1,0:T(8,128)S(1)}, f32[4,32,128]{2,1,0:T(8,128)}, u32[]{:S(2)}) copy-start(f32[4,32,128]{2,1,0:T(8,128)} %get-tuple-element.87) | copy-start | bytes 196612
  347.4 9.9 %copy-start.5 = (f32[4,32,128]{2,1,0:T(8,128)S(1)}, f32[4,32,128]{2,1,0:T(8,128)}, u32[]{:S(2)}) copy-start(f32[4,32,128]{2,1,0:T(8,128)} %get-tuple-element.88) | copy-start | bytes 196612
  347.4 9.9 %copy-start.6 = (f32[4,32,128]{2,1,0:T(8,128)S(1)}, f32[4,32,128]{2,1,0:T(8,128)}, u32[]{:S(2)}) copy-start(f32[4,32,128]{2,1,0:T(8,128)} %get-tuple-element.89) | copy-start | bytes 196612
  347.4 9.9 %copy-start.12 = (f32[3,4,32,128]{3,2,1,0:T(8,128)S(1)}, f32[3,4,32,128]{3,2,1,0:T(8,128)}, u32[]{:S(2)}) copy-start(f32[3,4,32,128]{3,2,1,0:T(8,128)} %param.13) | copy-start | bytes 589828
  347.4 9.8 %copy-start.17 = (f32[3]{0:T(128)S(1)}, f32[3]{0:T(128)}, u32[]{:S(2)}) copy-start(f32[3]{0:T(128)} %pad.6.clone) | copy-start | bytes 40
  347.6 8.8 %collective-permute-start.3 = (f32[2,4,32,1]{3,2,1,0:T(8,128)S(1)}, f32[2,4,32,1]{3,2,1,0:T(8,128)S(1)}, u32[]{:S(2)}, u32[]{:S(2)}) collective-permute-start(f32[2,4,32,1]{3,2,1,0:T(8,128)S(1)} %slice.175), channel_id=1, source_target_pairs={{0,2},{2,4},{4,6},{1,3},{3,5},{5,7},{8,10},{10,12},{12,14},{9,11},... | collective-permute-start | bytes 3080 | tf_op jit(solution)/shard_map/ppermute | solution.py:16
  351.3 5.1 %collective-permute-start.5 = (f32[2,4,1,128]{3,2,1,0:T(1,128)S(1)}, f32[2,4,1,128]{3,2,1,0:T(1,128)S(1)}, u32[]{:S(2)}, u32[]{:S(2)}) collective-permute-start(f32[2,4,1,128]{3,2,1,0:T(1,128)S(1)} %pad_maximum_fusion.2), channel_id=1, source_target_pairs={{0,8},{8,16},{16,24},{1,9},{9,17},{17,25},{2,10},{10,18},{18,26},{... | collective-permute-start | bytes 12296 | tf_op jit(solution)/shard_map/ppermute | solution.py:16
  354.7 2.4 collective-permute-start.4
Sparse Core Ops, SparseCore 0:
  25.0 26.6 all-gather.1
  329.4 14.9 all-reduce.1
where the time goes:
time: 368 us; the launch traced here: 365 us
  other arithmetic  123 us (33%)
  local copies, waits for them, and re-layouts  77.2 us (21%)
  matrix products  49.4 us (13%)
  blocking collectives  38.6 us (10%)
  loops' own time  34.3 us (9%)
  waiting for transfers between devices  15.1 us (4%)
  between operations  14.5 us (4%)
  starting transfers between devices  12.6 us (3%)
    cos x16, other arithmetic, one_freq(): right = jnp.concatenate([jnp.cos(phase_y), jnp.sin(phase_y)], axis=1).T  59 us
    dot_general x16, matrix products, one_freq(): jnp.dot(left, right, preferred_element_type=jnp.float32, precision=lax.Pr...  49.4 us
    another operation x1, loops' own time, surface_source(): lax.scan(one_freq, start, jnp.arange(cotangent.shape[0], dtype=jnp.int32))  34.3 us
    cos x16, other arithmetic, one_freq(): cos_x = jnp.cos(phase_x)[None]  26.9 us
    dynamic_slice x16, local copies, waits for them, and re-layouts, one_freq(): phase_x = xs[:, None] * along_x[None, :] - time_phase[freq]  21.1 us
    dynamic_slice x16, local copies, waits for them, and re-layouts, one_freq(): wave = wavenumber[freq]  21.1 us
    sub x16, other arithmetic, one_freq(): first = real_part * cos_x - imag_part * sin_x  20 us
    all_gather x1, blocking collectives, local(): lax.all_gather(cotangent, 'gx', axis=2, tiled=True)  17.6 us
  transfers between devices with their start and end apart: 8, of which 2 were waited for; matrix products, arithmetic and copies ran while one was open for 67% of the time, Pallas kernels for 0%

commit v1 on v0

--- a/solution.py
+++ b/solution.py
@@ -74,7 +74,7 @@
     )
     xs = anchor_x + jnp.arange(width_x).astype(jnp.float32)
     partial_value = surface_source(band_cot, band_cos, wavenumber, time_phase, xs, ys)
-    source = lax.psum(partial_value, "gz") * scale
+    source = jnp.sum(lax.all_gather(partial_value, "gz"), axis=0) * scale
     is_top = lax.axis_index("gz") == lax.axis_size("gz") - 1
     top = ((jnp.arange(depth) == depth - 1) & is_top).astype(jnp.float32)[:, None, None]
     next_x = from_behind(e_field[1:3, :, :1, :], "gx", -1)

time: 368 us -> 337 us (0.916)
  waiting for transfers between devices: 15.1 us -> 0.73 us
  loops' own time: 34.3 us -> 28.6 us
  other arithmetic: 123 us -> 118 us
  local copies, waits for them, and re-layouts: 77.2 us -> 72.5 us
    psum x1 -> x0, waiting for transfers between devices: 14.3 us -> none  [local(): source = lax.psum(partial_value, 'gz') * scale]
    another operation x1, loops' own time: 34.3 us -> 28.6 us  [surface_source(): lax.scan(one_freq, start, jnp.arange(cotangent.shape[0], dtype=jnp.int32))]
  transfers between devices with their start and end apart: 8 -> 7, of which waited for: 2 -> 1; matrix products, arithmetic and copies ran while one was open for 67% -> 3% of each run, Pallas kernels for 0% -> 0%
where the time goes in v1:
time: 337 us; the launch traced here: 334 us
  other arithmetic  118 us (35%)
  local copies, waits for them, and re-layouts  72.5 us (22%)
  matrix products  49.4 us (15%)
  blocking collectives  40.6 us (12%)
  loops' own time  28.6 us (8%)
  between operations  14.5 us (4%)
  starting transfers between devices  9.46 us (3%)
    cos x16, other arithmetic, one_freq(): right = jnp.concatenate([jnp.cos(phase_y), jnp.sin(phase_y)], axis=1).T  59 us
    dot_general x16, matrix products, one_freq(): jnp.dot(left, right, preferred_element_type=jnp.float32, precision=lax.Pr...  49.4 us
    another operation x1, loops' own time, surface_source(): lax.scan(one_freq, start, jnp.arange(cotangent.shape[0], dtype=jnp.int32))  28.6 us
    cos x16, other arithmetic, one_freq(): cos_x = jnp.cos(phase_x)[None]  25 us
    dynamic_slice x16, local copies, waits for them, and re-layouts, one_freq(): phase_x = xs[:, None] * along_x[None, :] - time_phase[freq]  19.9 us
    dynamic_slice x16, local copies, waits for them, and re-layouts, one_freq(): wave = wavenumber[freq]  19.9 us
    sub x16, other arithmetic, one_freq(): first = real_part * cos_x - imag_part * sin_x  19.6 us
    all_gather x1, blocking collectives, local(): lax.all_gather(cotangent, 'gx', axis=2, tiled=True)  17.6 us
  transfers between devices with their start and end apart: 7, of which 1 were waited for; matrix products, arithmetic and copies ran while one was open for 3% of the time, Pallas kernels for 0%

profile of v1, /device:TPU:0, one launch (start us, length us, event | category | flops | bytes accessed | tf_op | source)
XLA Modules:
  0.0 334.0 jit_solution(15388799746869980846)
XLA Ops:
  7.2 17.6 %all_gather.18 = f32[16,8,512]{2,1,0:T(8,128)} all-gather(f32[16,8,128]{2,1,0:T(8,128)} %param.16), channel_id=1, replica_groups=mesh['gx'=4,'gy'=4,'gz'=2] {'gx'}, dimensions={2}, use_global_device_ids=true | all-gather | bytes 327680 | tf_op jit(solution)/shard_map/all_gather | solution.py:68
  25.8 1.3 collective-permute-start.1
  27.9 1.3 collective-permute-start.2
  29.9 1.3 collective-permute-start
  32.2 10.5 %all_gather.20 = f32[2,512]{1,0:T(2,128)S(1)} all-gather(f32[2,128]{1,0:T(2,128)} %param.17), channel_id=1, replica_groups=mesh['gx'=4,'gy'=4,'gz'=2] {'gx'}, dimensions={1}, use_global_device_ids=true | all-gather | bytes 5120 | tf_op jit(solution)/shard_map/all_gather | solution.py:69
  42.8 10.4 %all_gather.21 = f32[2,2048]{1,0:T(2,128)S(1)} all-gather(f32[2,512]{1,0:T(2,128)S(1)} %all_gather.20), channel_id=1, replica_groups=mesh['gx'=4,'gy'=4,'gz'=2] {'gy'}, dimensions={1}, use_global_device_ids=true | all-gather | bytes 20480 | tf_op jit(solution)/shard_map/all_gather | solution.py:73
  54.0 1.7 select_reduce_fusion.2
  60.3 254.9 %while.11 = (s32[]{:T(128)}, f32[4,32,128]{2,1,0:T(8,128)S(1)}, s32[16]{0:T(128)S(1)}, f32[16,8,2048]{2,1,0:T(8,128)}, f32[16]{0:T(128)}, /*index=5*/f32[2,2048]...) while((s32[]{:T(128)}, f32[4,32,128]{2,1,0:T(8,128)S(1)}, ...), condition=%wide.region_2.3_spmd.clone, body=%wide.region_1.2_spmd.clone.sunk | while | flops 808620352 | bytes 9947153 | solution.py:45
  64.4 1.2 dynamic_slice.25
  65.7 1.6 fusion.56
  69.4 3.7 %multiply_cosine_fusion.2 = (f32[128,2048]{1,0:T(8,128)S(1)}, f32[128,2048]{1,0:T(8,128)S(1)}) fusion(f32[2048]{0:T(1024)S(1)} %bitcast.106, f32[128]{0:T(128)S(1)} %convert_add_fusion.4), kind=kLoop, calls=%fused_computation.10.clone.1 | loop fusion | flops 262144 | bytes 2105856 | tf_op jit(solution)/shard_map/while/body/eval_jaxpr/cos | solution.py:38
  73.1 3.1 fusion.57
  81.6 1.6 fusion.56
  85.3 3.7 %multiply_cosine_fusion.2 = (f32[128,2048]{1,0:T(8,128)S(1)}, f32[128,2048]{1,0:T(8,128)S(1)}) fusion(f32[2048]{0:T(1024)S(1)} %bitcast.106, f32[128]{0:T(128)S(1)} %convert_add_fusion.4), kind=kLoop, calls=%fused_computation.10.clone.1 | loop fusion | flops 262144 | bytes 2105856 | tf_op jit(solution)/shard_map/while/body/eval_jaxpr/cos | solution.py:38
  89.0 3.1 fusion.57
  96.3 1.2 dynamic_slice.25
  97.5 1.6 fusion.56
  101.2 3.7 %multiply_cosine_fusion.2 = (f32[128,2048]{1,0:T(8,128)S(1)}, f32[128,2048]{1,0:T(8,128)S(1)}) fusion(f32[2048]{0:T(1024)S(1)} %bitcast.106, f32[128]{0:T(128)S(1)} %convert_add_fusion.4), kind=kLoop, calls=%fused_computation.10.clone.1 | loop fusion | flops 262144 | bytes 2105856 | tf_op jit(solution)/shard_map/while/body/eval_jaxpr/cos | solution.py:38
  104.9 3.1 fusion.57
  112.2 1.2 dynamic_slice.25
  113.5 1.6 fusion.56
  117.2 3.7 %multiply_cosine_fusion.2 = (f32[128,2048]{1,0:T(8,128)S(1)}, f32[128,2048]{1,0:T(8,128)S(1)}) fusion(f32[2048]{0:T(1024)S(1)} %bitcast.106, f32[128]{0:T(128)S(1)} %convert_add_fusion.4), kind=kLoop, calls=%fused_computation.10.clone.1 | loop fusion | flops 262144 | bytes 2105856 | tf_op jit(solution)/shard_map/while/body/eval_jaxpr/cos | solution.py:38
  120.9 3.1 fusion.57
  128.1 1.2 dynamic_slice.25
  129.4 1.6 fusion.56
  133.1 3.7 %multiply_cosine_fusion.2 = (f32[128,2048]{1,0:T(8,128)S(1)}, f32[128,2048]{1,0:T(8,128)S(1)}) fusion(f32[2048]{0:T(1024)S(1)} %bitcast.106, f32[128]{0:T(128)S(1)} %convert_add_fusion.4), kind=kLoop, calls=%fused_computation.10.clone.1 | loop fusion | flops 262144 | bytes 2105856 | tf_op jit(solution)/shard_map/while/body/eval_jaxpr/cos | solution.py:38
  136.8 3.1 fusion.57
  145.3 1.6 fusion.56
  149.0 3.7 %multiply_cosine_fusion.2 = (f32[128,2048]{1,0:T(8,128)S(1)}, f32[128,2048]{1,0:T(8,128)S(1)}) fusion(f32[2048]{0:T(1024)S(1)} %bitcast.106, f32[128]{0:T(128)S(1)} %convert_add_fusion.4), kind=kLoop, calls=%fused_computation.10.clone.1 | loop fusion | flops 262144 | bytes 2105856 | tf_op jit(solution)/shard_map/while/body/eval_jaxpr/cos | solution.py:38
  152.7 3.1 fusion.57
  161.3 1.6 fusion.56
  165.0 3.7 %multiply_cosine_fusion.2 = (f32[128,2048]{1,0:T(8,128)S(1)}, f32[128,2048]{1,0:T(8,128)S(1)}) fusion(f32[2048]{0:T(1024)S(1)} %bitcast.106, f32[128]{0:T(128)S(1)} %convert_add_fusion.4), kind=kLoop, calls=%fused_computation.10.clone.1 | loop fusion | flops 262144 | bytes 2105856 | tf_op jit(solution)/shard_map/while/body/eval_jaxpr/cos | solution.py:38
  168.7 3.1 fusion.57
  177.2 1.6 fusion.56
  180.9 3.7 %multiply_cosine_fusion.2 = (f32[128,2048]{1,0:T(8,128)S(1)}, f32[128,2048]{1,0:T(8,128)S(1)}) fusion(f32[2048]{0:T(1024)S(1)} %bitcast.106, f32[128]{0:T(128)S(1)} %convert_add_fusion.4), kind=kLoop, calls=%fused_computation.10.clone.1 | loop fusion | flops 262144 | bytes 2105856 | tf_op jit(solution)/shard_map/while/body/eval_jaxpr/cos | solution.py:38
  184.6 3.1 fusion.57
  193.1 1.6 fusion.56
  196.8 3.7 %multiply_cosine_fusion.2 = (f32[128,2048]{1,0:T(8,128)S(1)}, f32[128,2048]{1,0:T(8,128)S(1)}) fusion(f32[2048]{0:T(1024)S(1)} %bitcast.106, f32[128]{0:T(128)S(1)} %convert_add_fusion.4), kind=kLoop, calls=%fused_computation.10.clone.1 | loop fusion | flops 262144 | bytes 2105856 | tf_op jit(solution)/shard_map/while/body/eval_jaxpr/cos | solution.py:38
  200.5 3.1 fusion.57
  209.1 1.6 fusion.56
  212.8 3.7 %multiply_cosine_fusion.2 = (f32[128,2048]{1,0:T(8,128)S(1)}, f32[128,2048]{1,0:T(8,128)S(1)}) fusion(f32[2048]{0:T(1024)S(1)} %bitcast.106, f32[128]{0:T(128)S(1)} %convert_add_fusion.4), kind=kLoop, calls=%fused_computation.10.clone.1 | loop fusion | flops 262144 | bytes 2105856 | tf_op jit(solution)/shard_map/while/body/eval_jaxpr/cos | solution.py:38
  216.5 3.1 fusion.57
  225.0 1.6 fusion.56
  228.7 3.7 %multiply_cosine_fusion.2 = (f32[128,2048]{1,0:T(8,128)S(1)}, f32[128,2048]{1,0:T(8,128)S(1)}) fusion(f32[2048]{0:T(1024)S(1)} %bitcast.106, f32[128]{0:T(128)S(1)} %convert_add_fusion.4), kind=kLoop, calls=%fused_computation.10.clone.1 | loop fusion | flops 262144 | bytes 2105856 | tf_op jit(solution)/shard_map/while/body/eval_jaxpr/cos | solution.py:38
  232.4 3.1 fusion.57
  240.9 1.6 fusion.56
  244.6 3.7 %multiply_cosine_fusion.2 = (f32[128,2048]{1,0:T(8,128)S(1)}, f32[128,2048]{1,0:T(8,128)S(1)}) fusion(f32[2048]{0:T(1024)S(1)} %bitcast.106, f32[128]{0:T(128)S(1)} %convert_add_fusion.4), kind=kLoop, calls=%fused_computation.10.clone.1 | loop fusion | flops 262144 | bytes 2105856 | tf_op jit(solution)/shard_map/while/body/eval_jaxpr/cos | solution.py:38
  248.3 3.1 fusion.57
  256.9 1.6 fusion.56
  260.6 3.7 %multiply_cosine_fusion.2 = (f32[128,2048]{1,0:T(8,128)S(1)}, f32[128,2048]{1,0:T(8,128)S(1)}) fusion(f32[2048]{0:T(1024)S(1)} %bitcast.106, f32[128]{0:T(128)S(1)} %convert_add_fusion.4), kind=kLoop, calls=%fused_computation.10.clone.1 | loop fusion | flops 262144 | bytes 2105856 | tf_op jit(solution)/shard_map/while/body/eval_jaxpr/cos | solution.py:38
  264.3 3.1 fusion.57
  272.8 1.6 fusion.56
  276.5 3.7 %multiply_cosine_fusion.2 = (f32[128,2048]{1,0:T(8,128)S(1)}, f32[128,2048]{1,0:T(8,128)S(1)}) fusion(f32[2048]{0:T(1024)S(1)} %bitcast.106, f32[128]{0:T(128)S(1)} %convert_add_fusion.4), kind=kLoop, calls=%fused_computation.10.clone.1 | loop fusion | flops 262144 | bytes 2105856 | tf_op jit(solution)/shard_map/while/body/eval_jaxpr/cos | solution.py:38
  280.2 3.1 fusion.57
  288.7 1.6 fusion.56
  292.4 3.7 %multiply_cosine_fusion.2 = (f32[128,2048]{1,0:T(8,128)S(1)}, f32[128,2048]{1,0:T(8,128)S(1)}) fusion(f32[2048]{0:T(1024)S(1)} %bitcast.106, f32[128]{0:T(128)S(1)} %convert_add_fusion.4), kind=kLoop, calls=%fused_computation.10.clone.1 | loop fusion | flops 262144 | bytes 2105856 | tf_op jit(solution)/shard_map/while/body/eval_jaxpr/cos | solution.py:38
  296.1 3.1 fusion.57
  304.7 1.6 fusion.56
  308.4 3.7 %multiply_cosine_fusion.2 = (f32[128,2048]{1,0:T(8,128)S(1)}, f32[128,2048]{1,0:T(8,128)S(1)}) fusion(f32[2048]{0:T(1024)S(1)} %bitcast.106, f32[128]{0:T(128)S(1)} %convert_add_fusion.4), kind=kLoop, calls=%fused_computation.10.clone.1 | loop fusion | flops 262144 | bytes 2105856 | tf_op jit(solution)/shard_map/while/body/eval_jaxpr/cos | solution.py:38
  312.1 3.1 fusion.57
  315.2 2.0 all-gather
  319.7 2.5 collective-permute-start.3
  322.2 1.6 collective-permute-start.5
  323.8 1.5 collective-permute-start.4
  (307 shorter events, 100.8 us)
Async XLA Ops:
  7.2 48.5 %copy-start = (f32[3,4,32,128]{3,2,1,0:T(8,128)S(1)}, f32[3,4,32,128]{3,2,1,0:T(8,128)}, u32[]{:S(2)}) copy-start(f32[3,4,32,128]{3,2,1,0:T(8,128)} %param.11) | copy-start | bytes 589828
  7.2 53.1 %all-gather.3.cloned.1.call-start = ((), (), s32[]{:S(2)}) async-start(), calls=%async_computation | async-start | bytes 1310720 | tf_op jit(solution)/shard_map/all_gather | solution.py:72
  25.8 32.5 %collective-permute-start.1 = (f32[2,4,32,1]{3,2,1,0:T(8,128)S(1)}, f32[2,4,32,1]{3,2,1,0:T(8,128)S(1)}, u32[]{:S(2)}, u32[]{:S(2)}) collective-permute-start(f32[2,4,32,1]{3,2,1,0:T(8,128)S(1)} %slice.159), channel_id=1, source_target_pairs={{2,0},{4,2},{6,4},{3,1},{5,3},{7,5},{10,8},{12,10},{14,12},{11,9},... | collective-permute-start | bytes 3080 | tf_op jit(solution)/shard_map/ppermute | solution.py:16
  27.9 31.8 %collective-permute-start.2 = (f32[2,1,32,128]{3,2,1,0:T(8,128)S(1)}, f32[2,1,32,128]{3,2,1,0:T(8,128)S(1)}, u32[]{:S(2)}, u32[]{:S(2)}) collective-permute-start(f32[2,1,32,128]{3,2,1,0:T(8,128)S(1)} %slice.166), channel_id=1, source_target_pairs={{1,0},{3,2},{5,4},{7,6},{9,8},{11,10},{13,12},{15,14},{17,16},{19,... | collective-permute-start | bytes 98312 | tf_op jit(solution)/shard_map/ppermute | solution.py:16
  29.9 29.1 %collective-permute-start = (f32[2,4,1,128]{3,2,1,0:T(1,128)S(1)}, f32[2,4,1,128]{3,2,1,0:T(1,128)S(1)}, u32[]{:S(2)}, u32[]{:S(2)}) collective-permute-start(f32[2,4,1,128]{3,2,1,0:T(1,128)S(1)} %slice.155), channel_id=1, source_target_pairs={{8,0},{16,8},{24,16},{9,1},{17,9},{25,17},{10,2},{18,10},{26,18},{... | collective-permute-start | bytes 12296 | tf_op jit(solution)/shard_map/ppermute | solution.py:16
  60.3 3.6 %copy-start.20 = (s32[16]{0:T(128)}, s32[16]{0:T(128)S(1)}, u32[]{:S(2)}) copy-start(s32[16]{0:T(128)S(1)} %get-tuple-element.269) | copy-start | bytes 196 | tf_op jit(solution)/shard_map/while
  73.1 3.1 copy-start.21
  76.2 3.6 %copy-start.20 = (s32[16]{0:T(128)}, s32[16]{0:T(128)S(1)}, u32[]{:S(2)}) copy-start(s32[16]{0:T(128)S(1)} %get-tuple-element.269) | copy-start | bytes 196 | tf_op jit(solution)/shard_map/while
  89.0 3.1 copy-start.21
  92.1 3.6 %copy-start.20 = (s32[16]{0:T(128)}, s32[16]{0:T(128)S(1)}, u32[]{:S(2)}) copy-start(s32[16]{0:T(128)S(1)} %get-tuple-element.269) | copy-start | bytes 196 | tf_op jit(solution)/shard_map/while
  104.9 3.1 copy-start.21
  108.1 3.6 %copy-start.20 = (s32[16]{0:T(128)}, s32[16]{0:T(128)S(1)}, u32[]{:S(2)}) copy-start(s32[16]{0:T(128)S(1)} %get-tuple-element.269) | copy-start | bytes 196 | tf_op jit(solution)/shard_map/while
  120.9 3.1 copy-start.21
  124.0 3.6 %copy-start.20 = (s32[16]{0:T(128)}, s32[16]{0:T(128)S(1)}, u32[]{:S(2)}) copy-start(s32[16]{0:T(128)S(1)} %get-tuple-element.269) | copy-start | bytes 196 | tf_op jit(solution)/shard_map/while
  136.8 3.1 copy-start.21
  139.9 3.6 %copy-start.20 = (s32[16]{0:T(128)}, s32[16]{0:T(128)S(1)}, u32[]{:S(2)}) copy-start(s32[16]{0:T(128)S(1)} %get-tuple-element.269) | copy-start | bytes 196 | tf_op jit(solution)/shard_map/while
  152.7 3.1 copy-start.21
  155.9 3.6 %copy-start.20 = (s32[16]{0:T(128)}, s32[16]{0:T(128)S(1)}, u32[]{:S(2)}) copy-start(s32[16]{0:T(128)S(1)} %get-tuple-element.269) | copy-start | bytes 196 | tf_op jit(solution)/shard_map/while
  168.7 3.1 copy-start.21
  171.8 3.6 %copy-start.20 = (s32[16]{0:T(128)}, s32[16]{0:T(128)S(1)}, u32[]{:S(2)}) copy-start(s32[16]{0:T(128)S(1)} %get-tuple-element.269) | copy-start | bytes 196 | tf_op jit(solution)/shard_map/while
  184.6 3.1 copy-start.21
  187.7 3.6 %copy-start.20 = (s32[16]{0:T(128)}, s32[16]{0:T(128)S(1)}, u32[]{:S(2)}) copy-start(s32[16]{0:T(128)S(1)} %get-tuple-element.269) | copy-start | bytes 196 | tf_op jit(solution)/shard_map/while
  200.5 3.1 copy-start.21
  203.7 3.6 %copy-start.20 = (s32[16]{0:T(128)}, s32[16]{0:T(128)S(1)}, u32[]{:S(2)}) copy-start(s32[16]{0:T(128)S(1)} %get-tuple-element.269) | copy-start | bytes 196 | tf_op jit(solution)/shard_map/while
  216.5 3.1 copy-start.21
  219.6 3.6 %copy-start.20 = (s32[16]{0:T(128)}, s32[16]{0:T(128)S(1)}, u32[]{:S(2)}) copy-start(s32[16]{0:T(128)S(1)} %get-tuple-element.269) | copy-start | bytes 196 | tf_op jit(solution)/shard_map/while
  232.4 3.1 copy-start.21
  235.5 3.6 %copy-start.20 = (s32[16]{0:T(128)}, s32[16]{0:T(128)S(1)}, u32[]{:S(2)}) copy-start(s32[16]{0:T(128)S(1)} %get-tuple-element.269) | copy-start | bytes 196 | tf_op jit(solution)/shard_map/while
  248.3 3.1 copy-start.21
  251.5 3.6 %copy-start.20 = (s32[16]{0:T(128)}, s32[16]{0:T(128)S(1)}, u32[]{:S(2)}) copy-start(s32[16]{0:T(128)S(1)} %get-tuple-element.269) | copy-start | bytes 196 | tf_op jit(solution)/shard_map/while
  264.3 3.1 copy-start.21
  267.4 3.6 %copy-start.20 = (s32[16]{0:T(128)}, s32[16]{0:T(128)S(1)}, u32[]{:S(2)}) copy-start(s32[16]{0:T(128)S(1)} %get-tuple-element.269) | copy-start | bytes 196 | tf_op jit(solution)/shard_map/while
  280.2 3.1 copy-start.21
  283.3 3.6 %copy-start.20 = (s32[16]{0:T(128)}, s32[16]{0:T(128)S(1)}, u32[]{:S(2)}) copy-start(s32[16]{0:T(128)S(1)} %get-tuple-element.269) | copy-start | bytes 196 | tf_op jit(solution)/shard_map/while
  296.1 3.1 copy-start.21
  299.3 3.6 %copy-start.20 = (s32[16]{0:T(128)}, s32[16]{0:T(128)S(1)}, u32[]{:S(2)}) copy-start(s32[16]{0:T(128)S(1)} %get-tuple-element.269) | copy-start | bytes 196 | tf_op jit(solution)/shard_map/while
  312.1 3.1 copy-start.21
  315.2 3.4 %copy-start.1 = (f32[3,4,32,128]{3,2,1,0:T(8,128)S(1)}, f32[3,4,32,128]{3,2,1,0:T(8,128)}, u32[]{:S(2)}) copy-start(f32[3,4,32,128]{3,2,1,0:T(8,128)} %param.12) | copy-start | bytes 589828
  315.2 3.4 %copy-start.7 = (f32[1,4,32,1]{3,2,1,0:T(8,128)S(1)}, f32[1,4,32,1]{3,2,1,0:T(8,128)}, u32[]{:S(2)}) copy-start(f32[1,4,32,1]{3,2,1,0:T(8,128)} %get-tuple-element.133) | copy-start | bytes 1540
  315.2 3.4 %copy-start.16 = (f32[1,4,1,128]{3,2,1,0:T(1,128)S(1)}, f32[1,4,1,128]{3,2,1,0:T(1,128)}, u32[]{:S(2)}) copy-start(f32[1,4,1,128]{3,2,1,0:T(1,128)} %get-tuple-element.160) | copy-start | bytes 6148
  317.3 1.5 copy-start.6
  318.4 0.8 copy-start.8
  318.4 0.9 copy-start.9
  318.4 0.9 copy-start.10
  318.5 0.9 copy-start.12
  318.5 0.9 copy-start.13
  318.5 0.9 copy-start.14
  318.5 0.9 copy-start.15
  318.5 0.9 copy-start.17
  318.8 0.8 copy-start.2
  318.8 6.5 %copy-start.19 = (f32[4]{0:T(128)S(1)}, f32[4]{0:T(128)}, u32[]{:S(2)}) copy-start(f32[4]{0:T(128)} %fusion.44) | copy-start | bytes 52
  319.5 6.8 %copy-start.3 = (f32[4,32,128]{2,1,0:T(8,128)S(1)}, f32[4,32,128]{2,1,0:T(8,128)}, u32[]{:S(2)}) copy-start(f32[4,32,128]{2,1,0:T(8,128)} %get-tuple-element.87) | copy-start | bytes 196612
  319.5 6.8 %copy-start.4 = (f32[4,32,128]{2,1,0:T(8,128)S(1)}, f32[4,32,128]{2,1,0:T(8,128)}, u32[]{:S(2)}) copy-start(f32[4,32,128]{2,1,0:T(8,128)} %get-tuple-element.88) | copy-start | bytes 196612
  319.5 6.8 %copy-start.5 = (f32[4,32,128]{2,1,0:T(8,128)S(1)}, f32[4,32,128]{2,1,0:T(8,128)}, u32[]{:S(2)}) copy-start(f32[4,32,128]{2,1,0:T(8,128)} %get-tuple-element.89) | copy-start | bytes 196612
  319.5 6.8 %copy-start.11 = (f32[3,4,32,128]{3,2,1,0:T(8,128)S(1)}, f32[3,4,32,128]{3,2,1,0:T(8,128)}, u32[]{:S(2)}) copy-start(f32[3,4,32,128]{3,2,1,0:T(8,128)} %param.13) | copy-start | bytes 589828
  319.5 6.8 %copy-start.18 = (f32[3]{0:T(128)S(1)}, f32[3]{0:T(128)}, u32[]{:S(2)}) copy-start(f32[3]{0:T(128)} %pad.6.clone) | copy-start | bytes 40
  319.7 5.7 %collective-permute-start.3 = (f32[2,4,32,1]{3,2,1,0:T(8,128)S(1)}, f32[2,4,32,1]{3,2,1,0:T(8,128)S(1)}, u32[]{:S(2)}, u32[]{:S(2)}) collective-permute-start(f32[2,4,32,1]{3,2,1,0:T(8,128)S(1)} %slice.175), channel_id=1, source_target_pairs={{0,2},{2,4},{4,6},{1,3},{3,5},{5,7},{8,10},{10,12},{12,14},{9,11},... | collective-permute-start | bytes 3080 | tf_op jit(solution)/shard_map/ppermute | solution.py:16
  322.2 3.2 collective-permute-start.5
  323.8 2.4 collective-permute-start.4
Sparse Core Ops, SparseCore 0:
  25.0 26.6 all-gather.2
